TPU v7x, 32 devices: a whole 2x2x4 slice. The times are simulated.
32 devices in a mesh: seq: 8 (over z, y), batch: 4 (over x, core).
Axes of the slice: x: 2, y: 2, z: 4, core: 2. Of those that a mesh axis runs over, the one named last changes fastest.
Arguments:
- signal: bfloat16 [4, 1024, 8192], P('batch', 'seq'), may hold values from -6 to 6
- out_grad: bfloat16 [4, 1024, 8192], P('batch', 'seq'), may hold values from -6 to 6
- residues: float32 [8, 8192], replicated, may hold values from -0.3 to 0.3
- log_rates: float32 [8, 512], replicated, as said below
Outputs:
- mixed: bfloat16 [4, 1024, 8192], P('batch', 'seq')
- grad_signal: bfloat16 [4, 1024, 8192], P('batch', 'seq')
- grad_residues: float32 [8, 8192], replicated
- grad_rates: float32 [8, 512], replicated
Inputs may be any that keep to these rules, and one draw needn't show every extreme that they name: Each decay rate exp(log_rates) lies between 0.2 / 1024 and 1 / 30.
All inputs are finite; a program needn't handle non-finite values.
Results may differ from a plain program's by a relative error of at most 0.0012.
Values sent between devices are 32-bit elements; how exact they have to be, the bound alone decides.
A program may use at most 384 MiB of HBM per device.

v0:
```python
import jax
import jax.numpy as jnp
from jax import lax
from jax.sharding import PartitionSpec as P

M = 8
GROUP = 16
HIGHEST = lax.Precision.HIGHEST
HIGHER = lax.Precision.HIGH


def carried_in(shard, axis, combine, identity, reverse):
    peers, index = (lax.axis_size(axis), lax.axis_index(axis))
    everything = jax.tree.map(lambda part: lax.all_gather(part, axis), shard)
    start = jax.tree.map(
        lambda part, zero: jnp.broadcast_to(jnp.asarray(zero, part.dtype), part.shape),
        shard,
        identity,
    )

    def lap(k, before):
        at = peers - 1 - k if reverse else k
        reached = at > index if reverse else at < index
        new = combine(before, jax.tree.map(lambda part: part[at], everything))
        return jax.tree.map(lambda a, b: jnp.where(reached, a, b), new, before)

    return lax.fori_loop(0, peers, lap, start)


def depthwise(values, kernel, padding, precision):
    return lax.conv_general_dilated(
        values,
        kernel[:, None, :],
        (1,),
        [padding],
        dimension_numbers=("NWC", "WIO", "NWC"),
        feature_group_count=values.shape[2],
        precision=precision,
        preferred_element_type=jnp.float32,
    )


def local(signal, out_grad, residues, log_rates):
    batch_rows, length, channels = signal.shape
    groups = log_rates.shape[1]
    decay_rate = jnp.exp(log_rates)
    offsets = jnp.arange(length + 1, dtype=jnp.float32)
    powers = jnp.exp(-decay_rate[None] * offsets[:, None, None])
    res_group = residues.reshape(M, groups, GROUP)
    kernel = jnp.einsum("kmg,mgi->kgi", powers[:length], res_group, precision=HIGHEST).reshape(
        length, channels
    )
    inputs = signal.astype(jnp.float32)
    cotangent = out_grad.astype(jnp.float32)
    local_out = depthwise(inputs, kernel[::-1], (length - 1, 0), HIGHER)
    local_grad = depthwise(cotangent, kernel, (0, length - 1), HIGHER)
    weights = jnp.stack([powers[:length], offsets[:length, None, None] * powers[:length]])
    starts_table = jnp.stack([powers[:length], offsets[1:, None, None] * powers[1:]])
    input_group = inputs.reshape(batch_rows, length, groups, GROUP)
    grad_group = cotangent.reshape(batch_rows, length, groups, GROUP)
    end_states = jnp.einsum("jsmg,bsgi->jbmgi", weights[:, ::-1], input_group, precision=HIGHER)
    start_sums = jnp.einsum("jtmg,btgi->jbmgi", starts_table, grad_group, precision=HIGHER)
    local_state = end_states[0]
    local_moment = end_states[1]
    start_state = start_sums[0]
    weighted_start = start_sums[1]
    first_pole = powers[1][None, :, :, None]
    start_plain = first_pole * start_state
    empty_state = jnp.zeros_like(local_state)
    span = jnp.full((), float(length), jnp.float32)
    no_span = jnp.zeros((), jnp.float32)

    def join_forward(earlier, later):
        decay = jnp.exp(-decay_rate * later[0])[None, :, :, None]
        return (
            earlier[0] + later[0],
            decay * earlier[1] + later[1],
            decay * (earlier[2] + later[0] * earlier[1]) + later[2],
        )

    def join_backward(earlier, later):
        decay = jnp.exp(-decay_rate * later[0])[None, :, :, None]
        return (earlier[0] + later[0], decay * earlier[1] + later[1])

    forward_out = carried_in(
        (span, local_state, local_moment),
        "seq",
        join_forward,
        (no_span, empty_state, empty_state),
        False,
    )
    carry_state = forward_out[1]
    carry_moment = forward_out[2]
    backward_out = carried_in(
        (span, start_state), "seq", join_backward, (no_span, empty_state), True
    )
    adjoint = backward_out[1]
    out_extra = jnp.einsum(
        "tmg,bmgi->btgi", powers[1:], res_group[None] * carry_state, precision=HIGHEST
    ).reshape(batch_rows, length, channels)
    grad_extra = jnp.einsum(
        "tmg,bmgi->btgi", powers[1:][::-1], res_group[None] * adjoint, precision=HIGHEST
    ).reshape(batch_rows, length, channels)
    mixed = (local_out + out_extra).astype(jnp.bfloat16)
    grad_signal = (local_grad + grad_extra).astype(jnp.bfloat16)
    lag_values = jnp.swapaxes(out_grad, 0, 1).reshape(1, length, batch_rows * channels)
    lag_kernel = jnp.swapaxes(signal, 0, 1).reshape(length, batch_rows * channels)
    lagged = depthwise(lag_values, lag_kernel, (0, length - 1), None)
    lag_sums = jnp.sum(lagged.reshape(length, batch_rows, groups, GROUP), axis=1)
    lag_terms = jnp.einsum("jkmg,kgi->jmgi", weights, lag_sums, precision=HIGHEST)
    residue_part = lag_terms[0] + jnp.sum(carry_state * start_plain, axis=0)
    moment_part = lag_terms[1] + jnp.sum(
        carry_state * weighted_start + carry_moment * start_plain, axis=0
    )
    rate_part = -decay_rate * jnp.sum(res_group * moment_part, axis=2)
    norm_factor = 1.0 / (batch_rows * lax.axis_size("batch") * length * lax.axis_size("seq"))
    grad_residues, grad_rates = lax.psum(
        (residue_part.reshape(M, channels) * norm_factor, rate_part * norm_factor), ("seq", "batch")
    )
    return (mixed, grad_signal, grad_residues, grad_rates)


def solution(mesh):
    placed = (P("batch", "seq", None), P("batch", "seq", None), P(), P())
    return jax.shard_map(
        local,
        mesh=mesh,
        in_specs=placed,
        out_specs=(P("batch", "seq", None), P("batch", "seq", None), P(), P()),
        check_vma=False,
    )
```

profile of v0, /device:TPU:0, one launch (start us, length us, event | category | flops | bytes accessed | tf_op | source)
XLA Modules:
  0.0 764.3 jit_solution(8605537450636845793)
XLA Ops:
  8.9 2.6 multiply_bitcast_fusion.1
  11.4 3.8 pad_maximum_fusion
  15.2 7.2 rev.10
  22.5 3.2 copy.110
  25.7 4.6 fusion.16
  30.2 2.2 fusion.34
  33.3 3.2 copy.120
  36.5 6.5 fusion.9
  43.0 3.6 copy.122
  48.0 3.7 slice.55
  52.4 2.0 broadcast_in_dim_reshape.7
  55.7 11.2 %fusion.23 = f32[512,128,16]{1,2,0:T(8,128)} fusion(f32[8,512,16]{2,1,0:T(8,128)S(1)} %reshape.109, f32[129,8,512]{0,1,2:T(8,128)} %copy-done), kind=kOutput, calls=%fused_computation.31 | convolution fusion | flops 100663296 | bytes 6553600 | tf_op jit(solution)/shard_map/kmg,mgi->kgi/dot_general | solution.py:50
  69.0 24.8 %all-reduce = f32[8]{0:T(128)} all-reduce(f32[8]{0:T(128)S(1)} %dynamic-update-slice), channel_id=1, replica_groups=mesh['seq'=8,'batch'=4] {'seq'}, use_global_device_ids=true, to_apply=%add | all-reduce | flops 8 | bytes 64
  93.7 62.1 %fusion.7 = f32[1,128,8192]{2,0,1:T(1,128)} fusion(bf16[128,1,8192]{2,0,1:T(8,128)(2,1)} %bitcast.133, bf16[1,128,8192]{2,1,0:T(8,128)(2,1)} %param.9), kind=kOutput, calls=%fused_computation.16 | convolution fusion | flops 135266304 | bytes 8388608 | tf_op jit(solution)/shard_map/conv_general_dilated | solution.py:31
  155.8 9.7 %copy.129 = f32[1,128,8192]{1,2,0:T(8,128)} copy(f32[1,128,8192]{2,0,1:T(1,128)} %fusion.7) | data formatting | bytes 8388608 | tf_op jit(solution)/shard_map/conv_general_dilated | solution.py:31
  165.5 12.2 %fusion.5 = f32[512,16,2,8]{1,3,2,0:T(8,128)} fusion(f32[128,512,16,1]{0,2,3,1:T(8,128)} %bitcast.123, f32[2,128,8,512]{1,2,3,0:T(8,128)} %get-tuple-element.514), kind=kOutput, calls=%fused_computation.14 | convolution fusion | flops 201326592 | bytes 8912896 | tf_op jit(solution)/shard_map/jkmg,kgi->jmgi/dot_general | solution.py:110
  177.6 3.7 copy.131
  181.3 2.2 copy.132
  183.6 2.4 rev.11
  186.0 9.6 %copy.119 = f32[128,1,8192]{2,1,0:T(1,128)} copy(f32[128,1,8192]{0,2,1:T(8,128)} %bitcast.121) | data formatting | bytes 8388608 | tf_op jit(solution)/shard_map/broadcast_in_dim;reshape | solution.py:33
  195.6 5.6 copy.108
  201.2 32.7 %rev.9 = f32[128,8192]{1,0:T(8,128)} reverse(f32[128,8192]{1,0:T(8,128)} %copy.108), dimensions={0} | reverse | bytes 8388608 | tf_op jit(solution)/shard_map/rev | solution.py:55
  233.9 6.6 broadcast_in_dim.16
  240.5 22.5 %all-gather.4.cloned.1.call-done = f32[8,1,8,512,16]{4,2,0,3,1:T(8,128)} async-done(((f32[1,1,8,512,16]{4,2,0,3,1:T(8,128)}), f32[8,1,8,512,16]{4,2,0,3,1:T(8,128)}) %all-gather.4.cloned.1.call-update) | async-done | bytes 2097168 | tf_op jit(solution)/shard_map/all_gather | solution.py:14
  263.0 10.3 %copy.113 = f32[8,1,8,512,16]{3,4,2,1,0:T(8,128)S(1)} copy(f32[8,1,8,512,16]{4,2,0,3,1:T(8,128)} %all-gather.4.cloned.1.call-done) | data formatting | bytes 4194304
  273.4 217.2 %all-gather.6.cloned.1.call-done = f32[8,1,8,512,16]{4,2,0,3,1:T(8,128)} async-done(((f32[1,1,8,512,16]{4,2,0,3,1:T(8,128)}), f32[8,1,8,512,16]{4,2,0,3,1:T(8,128)}) %all-gather.6.cloned.1.call-update) | async-done | bytes 2097168 | tf_op jit(solution)/shard_map/all_gather | solution.py:14
  490.6 10.9 %copy.114 = f32[8,1,8,512,16]{3,4,2,1,0:T(8,128)} copy(f32[8,1,8,512,16]{4,2,0,3,1:T(8,128)} %all-gather.6.cloned.1.call-done) | data formatting | bytes 4194304
  501.5 25.2 %while.34 = (s32[]{:T(128)}, f32[1,8,512,16]{2,3,1,0:T(8,128)S(1)}, f32[1,8,512,16]{2,3,1,0:T(8,128)S(1)}, s32[]{:T(128)}, f32[8]{0:T(128)S(1)}, /*index=5*/f32[...) while((s32[]{:T(128)}, f32[1,8,512,16]{2,3,1,0:T(8,128)S(1)}, ...), condition=%wide.region_1.2_spmd.clone, body=%wide.region_0.1_spmd.clone.sunk | while | flops 659460 | bytes 1622161 | solution.py:27
  502.8 1.9 fusion.44
  509.0 1.9 fusion.44
  512.1 1.9 fusion.44
  521.5 1.9 fusion.44
  526.7 2.0 copy.115
  530.8 1.9 copy.133
  532.7 4.0 mul.217
  536.7 3.3 all-gather.8.cloned.1.call-done
  540.0 19.6 %while.35 = (s32[]{:T(128)}, f32[1,8,512,16]{2,3,1,0:T(8,128)S(1)}, s32[]{:T(128)}, f32[8]{0:T(128)S(1)}, f32[1,8,512,1]{2,1,3,0:T(8,128)S(1)}, /*index=5*/f32[8...) while((s32[]{:T(128)}, f32[1,8,512,16]{2,3,1,0:T(8,128)S(1)}, s32[]{:T(128)}, ...), condition=%wide.region_3.4_spmd.clone, body=%wide.region_2.3_spmd.clone.sunk | while | flops 266248 | bytes 835771 | solution.py:27
  559.6 1.9 copy.124
  561.5 4.0 multiply_bitcast_fusion
  565.6 10.0 %fusion.19 = f32[512,16,128]{2,1,0:T(8,128)} fusion(f32[128,8,512]{0,1,2:T(8,128)S(1)} %copy-done.7, f32[8,512,16]{2,1,0:T(8,128)S(1)} %get-tuple-element.511), kind=kOutput, calls=%fused_computation.27 | convolution fusion | flops 100663296 | bytes 6553600 | tf_op jit(solution)/shard_map/tmg,bmgi->btgi/dot_general | solution.py:101
  575.6 9.8 %copy.126 = f32[1,128,8192]{2,0,1:T(1,128)} copy(f32[1,128,8192]{1,2,0:T(8,128)} %bitcast.124) | data formatting | bytes 8388608 | tf_op jit(solution)/shard_map/reshape | solution.py:103
  585.5 12.4 %fusion.21 = f32[512,16,128]{2,1,0:T(8,128)} fusion(f32[8,512,16]{2,1,0:T(8,128)S(1)} %copy-done.6, f32[129,8,512]{0,1,2:T(8,128)} %copy-done), kind=kOutput, calls=%fused_computation.29 | convolution fusion | flops 100663296 | bytes 6553600 | tf_op jit(solution)/shard_map/tmg,bmgi->btgi/dot_general | solution.py:98
  597.8 9.8 %copy.117 = f32[1,128,8192]{2,0,1:T(1,128)} copy(f32[1,128,8192]{1,2,0:T(8,128)} %bitcast.125) | data formatting | bytes 8388608 | tf_op jit(solution)/shard_map/reshape | solution.py:100
  607.7 47.8 %fusion.3 = bf16[1,128,8192]{2,0,1:T(2,128)(2,1)} fusion(f32[1,128,8192]{2,0,1:T(1,128)} %copy.126, f32[128,1,8192]{2,1,0:T(1,128)} %copy.119, bf16[1,128,8192]{2,1,0:T(8,128)(2,1)S(1)} %copy-done.16), kind=kOutput, calls=%fused_computation.9 | convolution fusion | flops 407896064 | bytes 12582912 | tf_op jit(solution)/shard_map/conv_general_dilated | solution.py:31
  655.5 46.6 %fusion.4 = bf16[1,128,8192]{2,0,1:T(2,128)(2,1)} fusion(f32[1,128,8192]{2,0,1:T(1,128)S(1)} %copy-done.12, f32[128,1,8192]{2,1,0:T(1,128)S(1)} %copy-done.11, bf16[1,128,8192]{2,1,0:T(8,128)(2,1)S(1)} %copy-done.17), kind=kOutput, calls=%fused_computation.11 | convolution fusion | flops 407896064 | bytes 12582912 | tf_op jit(solution)/shard_map/conv_general_dilated | solution.py:31
  702.2 43.2 %psum.15 = f32[8,512]{0,1:T(8,128)S(1)} all-reduce(f32[8,512]{0,1:T(8,128)S(1)} %multiply_multiply_fusion), channel_id=1, replica_groups=mesh['seq'=8,'batch'=4] {'seq','batch'}, use_global_device_ids=true, to_apply=%region_6.7 | all-reduce | flops 4096 | bytes 32768 | tf_op jit(solution)/shard_map/psum | solution.py:117
  746.1 5.9 copy.137
  752.0 3.6 copy.136
  (125 shorter events, 49.0 us)
Async XLA Ops:
  7.2 255.8 %all-gather.4.cloned.1.call-start = ((), (), s32[]{:S(2)}) async-start(), calls=%async_computation | async-start | bytes 18874368 | tf_op jit(solution)/shard_map/all_gather | solution.py:14
  8.1 3.4 copy-start.13
  8.7 2.7 copy-start
  32.5 458.1 %all-gather.6.cloned.1.call-start = ((), (), s32[]{:S(2)}) async-start(), calls=%async_computation.1 | async-start | bytes 18874368 | tf_op jit(solution)/shard_map/all_gather | solution.py:14
  33.3 506.8 %all-gather.8.cloned.1.call-start = ((), (), s32[]{:S(2)}) async-start(), calls=%async_computation.2 | async-start | bytes 2359296 | tf_op jit(solution)/shard_map/all_gather | solution.py:14
  43.0 8.6 %copy-start.19 = (f32[8,8192]{1,0:T(8,128)S(1)}, f32[8,8192]{1,0:T(8,128)}, u32[]{:S(2)}) copy-start(f32[8,8192]{1,0:T(8,128)} %param.10) | copy-start | bytes 786436
  46.6 5.1 copy-start.8
  47.4 708.2 %all-reduce.3.cloned.1.call-start = ((), (), s32[]{:S(2)}) async-start(), calls=%async_computation.3 | async-start | bytes 524288 | tf_op jit(solution)/shard_map/psum | solution.py:117
  55.7 11.2 %copy-start.23 = (u32[32]{0:T(128)S(1)}, u32[32]{0:T(128)}, u32[]{:S(2)}) copy-start(u32[32]{0:T(128)} %constant.98) | copy-start | bytes 388
  177.6 5.9 copy-start.5
  273.3 228.2 %copy-start.1 = (f32[1,8,512,16]{2,3,1,0:T(8,128)S(1)}, f32[1,8,512,16]{2,3,1,0:T(8,128)}, u32[]{:S(2)}) copy-start(f32[1,8,512,16]{2,3,1,0:T(8,128)} %custom-call) | copy-start | bytes 786436
  273.3 228.2 %copy-start.2 = (f32[1,8,512,16]{2,3,1,0:T(8,128)S(1)}, f32[1,8,512,16]{2,3,1,0:T(8,128)}, u32[]{:S(2)}) copy-start(f32[1,8,512,16]{2,3,1,0:T(8,128)} %custom-call.1) | copy-start | bytes 786436
  273.3 228.1 %copy-start.18 = (f32[1,8,512,1]{2,1,3,0:T(8,128)S(1)}, f32[1,8,512,1]{2,1,3,0:T(8,128)}, u32[]{:S(2)}) copy-start(f32[1,8,512,1]{2,1,3,0:T(8,128)} %copy.112) | copy-start | bytes 49156
  273.3 228.1 %copy-start.22 = (f32[8]{0:T(128)S(1)}, f32[8]{0:T(128)}, u32[]{:S(2)}) copy-start(f32[8]{0:T(128)} %all-reduce) | copy-start | bytes 100
  501.5 27.2 %copy-start.9 = (f32[512,2,8,16]{0,3,2,1:T(8,128)S(1)}, f32[512,2,8,16]{0,3,2,1:T(8,128)}, u32[]{:S(2)}) copy-start(f32[512,2,8,16]{0,3,2,1:T(8,128)} %copy-done.8) | copy-start | bytes 1572868
  501.5 27.2 %copy-start.20 = (f32[8,512,16]{1,2,0:T(8,128)S(1)}, f32[8,512,16]{1,2,0:T(8,128)}, u32[]{:S(2)}) copy-start(f32[8,512,16]{1,2,0:T(8,128)} %copy.134) | copy-start | bytes 786436
  526.7 4.0 copy-start.15
  528.7 11.3 %copy-start.3 = (f32[1,8,512,16]{2,3,1,0:T(8,128)S(1)}, f32[1,8,512,16]{2,3,1,0:T(8,128)}, u32[]{:S(2)}) copy-start(f32[1,8,512,16]{2,3,1,0:T(8,128)} %custom-call.2) | copy-start | bytes 786436
  532.7 28.8 %copy-start.4 = (f32[1,8,512,16]{3,2,1,0:T(8,128)S(1)}, f32[1,8,512,16]{3,2,1,0:T(8,128)}, u32[]{:S(2)}) copy-start(f32[1,8,512,16]{3,2,1,0:T(8,128)} %broadcast_in_dim_reshape.7) | copy-start | bytes 786436
  561.5 4.0 copy-start.7
  575.6 9.8 %copy-start.6 = (f32[8,512,16]{2,1,0:T(8,128)S(1)}, f32[8,512,16]{2,1,0:T(8,128)}, u32[]{:S(2)}) copy-start(f32[8,512,16]{2,1,0:T(8,128)} %get-tuple-element.512) | copy-start | bytes 786436
  597.8 9.8 %copy-start.16 = (bf16[1,128,8192]{2,1,0:T(8,128)(2,1)S(1)}, bf16[1,128,8192]{2,1,0:T(8,128)(2,1)}, u32[]{:S(2)}) copy-start(bf16[1,128,8192]{2,1,0:T(8,128)(2,1)} %param.9) | copy-start | bytes 6291460
  607.7 47.8 %copy-start.11 = (f32[128,1,8192]{2,1,0:T(1,128)S(1)}, f32[128,1,8192]{2,1,0:T(1,128)}, u32[]{:S(2)}) copy-start(f32[128,1,8192]{2,1,0:T(1,128)} %broadcast_in_dim.16) | copy-start | bytes 12582916
  607.7 47.8 %copy-start.12 = (f32[1,128,8192]{2,0,1:T(1,128)S(1)}, f32[1,128,8192]{2,0,1:T(1,128)}, u32[]{:S(2)}) copy-start(f32[1,128,8192]{2,0,1:T(1,128)} %copy.117) | copy-start | bytes 12582916
  607.7 47.8 %copy-start.17 = (bf16[1,128,8192]{2,1,0:T(8,128)(2,1)S(1)}, bf16[1,128,8192]{2,1,0:T(8,128)(2,1)}, u32[]{:S(2)}) copy-start(bf16[1,128,8192]{2,1,0:T(8,128)(2,1)} %param.8) | copy-start | bytes 6291460
  655.5 46.6 %copy-start.14 = (f32[8,512]{0,1:T(8,128)S(1)}, f32[8,512]{0,1:T(8,128)}, u32[]{:S(2)}) copy-start(f32[8,512]{0,1:T(8,128)} %copy-done.13) | copy-start | bytes 49156
  655.5 46.6 %copy-start.21 = (f32[8,512]{0,1:T(8,128)S(1)}, f32[8,512]{0,1:T(8,128)}, u32[]{:S(2)}) copy-start(f32[8,512]{0,1:T(8,128)} %copy.142) | copy-start | bytes 49156
  746.1 6.0 copy-start.10
Sparse Core Ops, SparseCore 0:
  32.6 230.3 all-gather.3
  265.1 225.4 all-gather.5
  492.7 47.2 all-gather.7
  545.4 125.0 all-reduce.2
where the time goes:
time: 776 us; the launch traced here: 764 us
  waiting for transfers between devices  244 us (31%)
  matrix products  213 us (27%)
  local copies, waits for them, and re-layouts  176 us (23%)
  blocking collectives  68 us (9%)
  other arithmetic  47 us (6%)
  between operations  14.6 us (2%)
    all_gather x3, waiting for transfers between devices, carried_in(): everything = jax.tree.map(lambda part: lax.all_gather(part, axis), shard)  243 us
    conv_general_dilated x3, matrix products, depthwise(): lax.conv_general_dilated(values, kernel[:, None, :], (1,), [padding], dim...  156 us
    psum x1, blocking collectives, local(): lax.psum((residue_part.reshape(M, channels) * norm_factor, rate_part * no...  43.2 us
    unnamed x61, local copies, waits for them, and re-layouts  42.5 us
    rev x1, local copies, waits for them, and re-layouts, local(): local_out = depthwise(inputs, kernel[::-1], (length - 1, 0), HIGHER)  32.7 us
    unnamed x1, blocking collectives  24.8 us
    select_n x16, other arithmetic, lap(): return jax.tree.map(lambda a, b: jnp.where(reached, a, b), new, before)  24.2 us
  transfers between devices with their start and end apart: 4, of which 3 were waited for; matrix products, arithmetic and copies ran while one was open for 54% of the time, Pallas kernels for 0%

commit v1 on v0

--- a/solution.py
+++ b/solution.py
@@ -114,8 +114,12 @@
     )
     rate_part = -decay_rate * jnp.sum(res_group * moment_part, axis=2)
     norm_factor = 1.0 / (batch_rows * lax.axis_size("batch") * length * lax.axis_size("seq"))
-    grad_residues, grad_rates = lax.psum(
-        (residue_part.reshape(M, channels) * norm_factor, rate_part * norm_factor), ("seq", "batch")
+    grad_residues, grad_rates = jax.lax.psum(
+        jax.lax.psum(
+            (residue_part.reshape(M, channels) * norm_factor, rate_part * norm_factor),
+            axis_name="seq",
+        ),
+        axis_name="batch",
     )
     return (mixed, grad_signal, grad_residues, grad_rates)
 

time: 776 us -> 784 us (1.010)
    psum x1 -> x2, blocking collectives: 43.2 us -> 50.7 us  [the longest x1 37.8 us: local(): jax.lax.psum((residue_part.reshape(M, channels) * norm_factor, rate_part...]
    unnamed x61 -> x73, local copies, waits for them, and re-layouts: 42.5 us -> 41.9 us
  transfers between devices with their start and end apart: 4 -> 5, of which waited for: 3 -> 3; matrix products, arithmetic and copies ran while one was open for 54% -> 53% of each run, Pallas kernels for 0% -> 0%
where the time goes in v1:
time: 784 us; the launch traced here: 772 us
  waiting for transfers between devices  245 us (31%)
  matrix products  213 us (27%)
  local copies, waits for them, and re-layouts  176 us (22%)
  blocking collectives  75.4 us (10%)
  other arithmetic  47 us (6%)
  between operations  14.7 us (2%)
    all_gather x3, waiting for transfers between devices, carried_in(): everything = jax.tree.map(lambda part: lax.all_gather(part, axis), shard)  244 us
    conv_general_dilated x3, matrix products, depthwise(): lax.conv_general_dilated(values, kernel[:, None, :], (1,), [padding], dim...  157 us
    unnamed x73, local copies, waits for them, and re-layouts  41.9 us
    psum x1, blocking collectives, local(): jax.lax.psum((residue_part.reshape(M, channels) * norm_factor, rate_part...  37.8 us
    rev x1, local copies, waits for them, and re-layouts, local(): local_out = depthwise(inputs, kernel[::-1], (length - 1, 0), HIGHER)  32.7 us
    unnamed x1, blocking collectives  24.7 us
    select_n x16, other arithmetic, lap(): return jax.tree.map(lambda a, b: jnp.where(reached, a, b), new, before)  24.2 us
  transfers between devices with their start and end apart: 5, of which 3 were waited for; matrix products, arithmetic and copies ran while one was open for 53% of the time, Pallas kernels for 0%

profile of v1, /device:TPU:0, one launch (start us, length us, event | category | flops | bytes accessed | tf_op | source)
XLA Modules:
  0.0 772.4 jit_solution(12606575729807733718)
XLA Ops:
  8.9 2.6 multiply_bitcast_fusion.1
  11.4 3.8 pad_maximum_fusion
  15.2 7.2 rev.10
  22.5 3.2 copy.110
  25.7 4.6 fusion.16
  30.3 2.2 fusion.34
  33.3 3.2 copy.120
  36.5 6.5 fusion.9
  43.0 3.6 copy.122
  48.0 3.7 slice.55
  52.4 2.0 broadcast_in_dim_reshape.7
  55.7 11.2 %fusion.23 = f32[512,128,16]{1,2,0:T(8,128)} fusion(f32[8,512,16]{2,1,0:T(8,128)S(1)} %reshape.109, f32[129,8,512]{0,1,2:T(8,128)} %copy-done), kind=kOutput, calls=%fused_computation.31 | convolution fusion | flops 100663296 | bytes 6553600 | tf_op jit(solution)/shard_map/kmg,mgi->kgi/dot_general | solution.py:50
  69.0 24.7 %all-reduce = f32[8]{0:T(128)} all-reduce(f32[8]{0:T(128)S(1)} %dynamic-update-slice), channel_id=1, replica_groups=mesh['seq'=8,'batch'=4] {'seq'}, use_global_device_ids=true, to_apply=%add | all-reduce | flops 8 | bytes 64
  93.6 62.1 %fusion.7 = f32[1,128,8192]{2,0,1:T(1,128)} fusion(bf16[128,1,8192]{2,0,1:T(8,128)(2,1)} %bitcast.133, bf16[1,128,8192]{2,1,0:T(8,128)(2,1)} %param.9), kind=kOutput, calls=%fused_computation.16 | convolution fusion | flops 135266304 | bytes 8388608 | tf_op jit(solution)/shard_map/conv_general_dilated | solution.py:31
  155.7 9.7 %copy.129 = f32[1,128,8192]{1,2,0:T(8,128)} copy(f32[1,128,8192]{2,0,1:T(1,128)} %fusion.7) | data formatting | bytes 8388608 | tf_op jit(solution)/shard_map/conv_general_dilated | solution.py:31
  165.4 12.2 %fusion.5 = f32[512,16,2,8]{1,3,2,0:T(8,128)} fusion(f32[128,512,16,1]{0,2,3,1:T(8,128)} %bitcast.123, f32[2,128,8,512]{1,2,3,0:T(8,128)} %get-tuple-element.514), kind=kOutput, calls=%fused_computation.14 | convolution fusion | flops 201326592 | bytes 8912896 | tf_op jit(solution)/shard_map/jkmg,kgi->jmgi/dot_general | solution.py:110
  177.5 3.7 copy.131
  181.2 2.2 copy.132
  183.5 2.4 rev.11
  185.8 9.7 %copy.119 = f32[128,1,8192]{2,1,0:T(1,128)} copy(f32[128,1,8192]{0,2,1:T(8,128)} %bitcast.121) | data formatting | bytes 8388608 | tf_op jit(solution)/shard_map/broadcast_in_dim;reshape | solution.py:33
  195.5 5.6 copy.108
  201.1 32.7 %rev.9 = f32[128,8192]{1,0:T(8,128)} reverse(f32[128,8192]{1,0:T(8,128)} %copy.108), dimensions={0} | reverse | bytes 8388608 | tf_op jit(solution)/shard_map/rev | solution.py:55
  233.8 6.6 broadcast_in_dim.16
  240.4 22.7 %all-gather.4.cloned.1.call-done = f32[8,1,8,512,16]{4,2,0,3,1:T(8,128)} async-done(((f32[1,1,8,512,16]{4,2,0,3,1:T(8,128)}), f32[8,1,8,512,16]{4,2,0,3,1:T(8,128)}) %all-gather.4.cloned.1.call-update) | async-done | bytes 2097168 | tf_op jit(solution)/shard_map/all_gather | solution.py:14
  263.0 10.3 %copy.113 = f32[8,1,8,512,16]{3,4,2,1,0:T(8,128)S(1)} copy(f32[8,1,8,512,16]{4,2,0,3,1:T(8,128)} %all-gather.4.cloned.1.call-done) | data formatting | bytes 4194304
  273.4 217.2 %all-gather.6.cloned.1.call-done = f32[8,1,8,512,16]{4,2,0,3,1:T(8,128)} async-done(((f32[1,1,8,512,16]{4,2,0,3,1:T(8,128)}), f32[8,1,8,512,16]{4,2,0,3,1:T(8,128)}) %all-gather.6.cloned.1.call-update) | async-done | bytes 2097168 | tf_op jit(solution)/shard_map/all_gather | solution.py:14
  490.6 10.9 %copy.114 = f32[8,1,8,512,16]{3,4,2,1,0:T(8,128)} copy(f32[8,1,8,512,16]{4,2,0,3,1:T(8,128)} %all-gather.6.cloned.1.call-done) | data formatting | bytes 4194304
  501.5 25.0 %while.34 = (s32[]{:T(128)}, f32[1,8,512,16]{2,3,1,0:T(8,128)S(1)}, f32[1,8,512,16]{2,3,1,0:T(8,128)S(1)}, s32[]{:T(128)}, f32[8]{0:T(128)S(1)}, /*index=5*/f32[...) while((s32[]{:T(128)}, f32[1,8,512,16]{2,3,1,0:T(8,128)S(1)}, ...), condition=%wide.region_1.2_spmd.clone, body=%wide.region_0.1_spmd.clone.sunk | while | flops 659460 | bytes 1622161 | solution.py:27
  505.9 1.9 fusion.44
  509.0 1.9 fusion.44
  521.5 1.9 fusion.44
  526.5 2.0 copy.115
  529.5 1.9 copy.133
  531.5 4.0 mul.217
  535.6 4.4 all-gather.8.cloned.1.call-done
  540.0 19.8 %while.35 = (s32[]{:T(128)}, f32[1,8,512,16]{2,3,1,0:T(8,128)S(1)}, s32[]{:T(128)}, f32[8]{0:T(128)S(1)}, f32[1,8,512,1]{2,1,3,0:T(8,128)S(1)}, /*index=5*/f32[8...) while((s32[]{:T(128)}, f32[1,8,512,16]{2,3,1,0:T(8,128)S(1)}, s32[]{:T(128)}, ...), condition=%wide.region_3.4_spmd.clone, body=%wide.region_2.3_spmd.clone.sunk | while | flops 266248 | bytes 835771 | solution.py:27
  559.8 1.9 copy.124
  561.8 4.1 multiply_bitcast_fusion
  565.8 10.0 %fusion.19 = f32[512,16,128]{2,1,0:T(8,128)} fusion(f32[128,8,512]{0,1,2:T(8,128)S(1)} %copy-done.11, f32[8,512,16]{2,1,0:T(8,128)S(1)} %get-tuple-element.511), kind=kOutput, calls=%fused_computation.27 | convolution fusion | flops 100663296 | bytes 6553600 | tf_op jit(solution)/shard_map/tmg,bmgi->btgi/dot_general | solution.py:101
  575.8 9.8 %copy.126 = f32[1,128,8192]{2,0,1:T(1,128)} copy(f32[1,128,8192]{1,2,0:T(8,128)} %bitcast.124) | data formatting | bytes 8388608 | tf_op jit(solution)/shard_map/reshape | solution.py:103
  585.6 12.1 %fusion.21 = f32[512,16,128]{2,1,0:T(8,128)} fusion(f32[8,512,16]{2,1,0:T(8,128)S(1)} %copy-done.10, f32[129,8,512]{0,1,2:T(8,128)} %copy-done), kind=kOutput, calls=%fused_computation.29 | convolution fusion | flops 100663296 | bytes 6553600 | tf_op jit(solution)/shard_map/tmg,bmgi->btgi/dot_general | solution.py:98
  597.7 9.8 %copy.117 = f32[1,128,8192]{2,0,1:T(1,128)} copy(f32[1,128,8192]{1,2,0:T(8,128)} %bitcast.125) | data formatting | bytes 8388608 | tf_op jit(solution)/shard_map/reshape | solution.py:100
  607.6 47.8 %fusion.3 = bf16[1,128,8192]{2,0,1:T(2,128)(2,1)} fusion(f32[1,128,8192]{2,0,1:T(1,128)} %copy.126, f32[128,1,8192]{2,1,0:T(1,128)} %copy.119, bf16[1,128,8192]{2,1,0:T(8,128)(2,1)S(1)} %copy-done.21), kind=kOutput, calls=%fused_computation.9 | convolution fusion | flops 407896064 | bytes 12582912 | tf_op jit(solution)/shard_map/conv_general_dilated | solution.py:31
  655.4 46.8 %fusion.4 = bf16[1,128,8192]{2,0,1:T(2,128)(2,1)} fusion(f32[1,128,8192]{2,0,1:T(1,128)S(1)} %copy-done.17, f32[128,1,8192]{2,1,0:T(1,128)S(1)} %copy-done.16, bf16[1,128,8192]{2,1,0:T(8,128)(2,1)S(1)} %copy-done.22), kind=kOutput, calls=%fused_computation.11 | convolution fusion | flops 407896064 | bytes 12582912 | tf_op jit(solution)/shard_map/conv_general_dilated | solution.py:31
  702.8 37.8 %psum.30 = f32[8,512]{0,1:T(8,128)S(1)} all-reduce(f32[8,512]{0,1:T(8,128)S(1)} %multiply_multiply_fusion), channel_id=1, replica_groups=mesh['seq'=8,'batch'=4] {'seq'}, use_global_device_ids=true, to_apply=%region_7.8 | all-reduce | flops 4096 | bytes 32768 | tf_op jit(solution)/shard_map/psum | solution.py:118
  740.6 12.8 %psum.31 = f32[8,512]{0,1:T(8,128)S(1)} all-reduce(f32[8,512]{0,1:T(8,128)S(1)} %psum.30), channel_id=1, replica_groups=mesh['seq'=8,'batch'=4] {'batch'}, use_global_device_ids=true, to_apply=%region_8.9 | all-reduce | flops 4096 | bytes 32768 | tf_op jit(solution)/shard_map/psum | solution.py:117
  754.2 5.9 copy.137
  760.1 3.6 copy.136
  (141 shorter events, 50.3 us)
Async XLA Ops:
  7.2 255.9 %all-gather.4.cloned.1.call-start = ((), (), s32[]{:S(2)}) async-start(), calls=%async_computation | async-start | bytes 18874368 | tf_op jit(solution)/shard_map/all_gather | solution.py:14
  8.1 3.4 copy-start.18
  8.7 2.7 copy-start
  32.5 458.1 %all-gather.6.cloned.1.call-start = ((), (), s32[]{:S(2)}) async-start(), calls=%async_computation.1 | async-start | bytes 18874368 | tf_op jit(solution)/shard_map/all_gather | solution.py:14
  33.3 506.8 %all-gather.8.cloned.1.call-start = ((), (), s32[]{:S(2)}) async-start(), calls=%async_computation.2 | async-start | bytes 2359296 | tf_op jit(solution)/shard_map/all_gather | solution.py:14
  43.0 8.6 %copy-start.24 = (f32[8,8192]{1,0:T(8,128)S(1)}, f32[8,8192]{1,0:T(8,128)}, u32[]{:S(2)}) copy-start(f32[8,8192]{1,0:T(8,128)} %param.10) | copy-start | bytes 786436
  46.6 5.1 copy-start.12
  47.4 655.3 %all-reduce.4.cloned.1.call-start = ((), (), s32[]{:S(2)}) async-start(), calls=%async_computation.3 | async-start | bytes 524288 | tf_op jit(solution)/shard_map/psum | solution.py:118
  55.7 11.2 %copy-start.29 = (u32[32]{0:T(128)S(1)}, u32[32]{0:T(128)}, u32[]{:S(2)}) copy-start(u32[32]{0:T(128)} %constant.98) | copy-start | bytes 388
  177.5 5.9 copy-start.9
  183.4 345.1 %copy-start.26 = (f32[1,8,512]{2,1,0:T(8,128)}, f32[1,8,512]{2,1,0:T(8,128)S(1)}, u32[]{:S(2)}) copy-start(f32[1,8,512]{2,1,0:T(8,128)S(1)} %copy.132) | copy-start | bytes 49156
  273.3 228.2 %copy-start.1 = (f32[1,8,512,16]{2,3,1,0:T(8,128)S(1)}, f32[1,8,512,16]{2,3,1,0:T(8,128)}, u32[]{:S(2)}) copy-start(f32[1,8,512,16]{2,3,1,0:T(8,128)} %custom-call) | copy-start | bytes 786436
  273.3 228.2 %copy-start.4 = (f32[1,8,512,16]{2,3,1,0:T(8,128)S(1)}, f32[1,8,512,16]{2,3,1,0:T(8,128)}, u32[]{:S(2)}) copy-start(f32[1,8,512,16]{2,3,1,0:T(8,128)} %custom-call.1) | copy-start | bytes 786436
  273.4 228.1 %copy-start.23 = (f32[1,8,512,1]{2,1,3,0:T(8,128)S(1)}, f32[1,8,512,1]{2,1,3,0:T(8,128)}, u32[]{:S(2)}) copy-start(f32[1,8,512,1]{2,1,3,0:T(8,128)} %copy.112) | copy-start | bytes 49156
  273.4 228.1 %copy-start.28 = (f32[8]{0:T(128)S(1)}, f32[8]{0:T(128)}, u32[]{:S(2)}) copy-start(f32[8]{0:T(128)} %all-reduce) | copy-start | bytes 100
  501.5 27.0 %copy-start.13 = (f32[512,2,8,16]{0,3,2,1:T(8,128)S(1)}, f32[512,2,8,16]{0,3,2,1:T(8,128)}, u32[]{:S(2)}) copy-start(f32[512,2,8,16]{0,3,2,1:T(8,128)} %copy-done.12) | copy-start | bytes 1572868
  526.5 9.0 %copy-start.2 = (f32[1,8,512,16]{2,3,1,0:T(8,128)}, f32[1,8,512,16]{2,3,1,0:T(8,128)S(1)}, u32[]{:S(2)}) copy-start(f32[1,8,512,16]{2,3,1,0:T(8,128)S(1)} %get-tuple-element.352) | copy-start | bytes 786436
  526.5 9.0 %copy-start.5 = (f32[1,8,512,16]{2,3,1,0:T(8,128)}, f32[1,8,512,16]{2,3,1,0:T(8,128)S(1)}, u32[]{:S(2)}) copy-start(f32[1,8,512,16]{2,3,1,0:T(8,128)S(1)} %get-tuple-element.354) | copy-start | bytes 786436
  526.5 13.5 %copy-start.7 = (f32[1,8,512,16]{2,3,1,0:T(8,128)S(1)}, f32[1,8,512,16]{2,3,1,0:T(8,128)}, u32[]{:S(2)}) copy-start(f32[1,8,512,16]{2,3,1,0:T(8,128)} %custom-call.2) | copy-start | bytes 786436
  531.5 30.3 %copy-start.8 = (f32[1,8,512,16]{3,2,1,0:T(8,128)S(1)}, f32[1,8,512,16]{3,2,1,0:T(8,128)}, u32[]{:S(2)}) copy-start(f32[1,8,512,16]{3,2,1,0:T(8,128)} %broadcast_in_dim_reshape.7) | copy-start | bytes 786436
  535.5 228.2 %all-reduce.6.cloned.1.call-start = ((), (), s32[]{:S(2)}) async-start(), calls=%async_computation.4 | async-start | bytes 524288 | tf_op jit(solution)/shard_map/psum | solution.py:117
  561.8 4.1 copy-start.11
  575.8 9.8 %copy-start.10 = (f32[8,512,16]{2,1,0:T(8,128)S(1)}, f32[8,512,16]{2,1,0:T(8,128)}, u32[]{:S(2)}) copy-start(f32[8,512,16]{2,1,0:T(8,128)} %get-tuple-element.512) | copy-start | bytes 786436
  597.7 9.8 %copy-start.21 = (bf16[1,128,8192]{2,1,0:T(8,128)(2,1)S(1)}, bf16[1,128,8192]{2,1,0:T(8,128)(2,1)}, u32[]{:S(2)}) copy-start(bf16[1,128,8192]{2,1,0:T(8,128)(2,1)} %param.9) | copy-start | bytes 6291460
  607.6 47.8 %copy-start.16 = (f32[128,1,8192]{2,1,0:T(1,128)S(1)}, f32[128,1,8192]{2,1,0:T(1,128)}, u32[]{:S(2)}) copy-start(f32[128,1,8192]{2,1,0:T(1,128)} %broadcast_in_dim.16) | copy-start | bytes 12582916
  607.6 47.8 %copy-start.17 = (f32[1,128,8192]{2,0,1:T(1,128)S(1)}, f32[1,128,8192]{2,0,1:T(1,128)}, u32[]{:S(2)}) copy-start(f32[1,128,8192]{2,0,1:T(1,128)} %copy.117) | copy-start | bytes 12582916
  607.6 47.8 %copy-start.22 = (bf16[1,128,8192]{2,1,0:T(8,128)(2,1)S(1)}, bf16[1,128,8192]{2,1,0:T(8,128)(2,1)}, u32[]{:S(2)}) copy-start(bf16[1,128,8192]{2,1,0:T(8,128)(2,1)} %param.8) | copy-start | bytes 6291460
  655.4 46.9 %copy-start.3 = (f32[1,8,512,16]{2,3,1,0:T(8,128)S(1)}, f32[1,8,512,16]{2,3,1,0:T(8,128)}, u32[]{:S(2)}) copy-start(f32[1,8,512,16]{2,3,1,0:T(8,128)} %copy-done.2) | copy-start | bytes 786436
  655.4 46.9 %copy-start.6 = (f32[1,8,512,16]{2,3,1,0:T(8,128)S(1)}, f32[1,8,512,16]{2,3,1,0:T(8,128)}, u32[]{:S(2)}) copy-start(f32[1,8,512,16]{2,3,1,0:T(8,128)} %copy-done.5) | copy-start | bytes 786436
  655.4 46.9 %copy-start.14 = (f32[512,2,8,16]{0,3,2,1:T(8,128)S(1)}, f32[512,2,8,16]{0,3,2,1:T(8,128)}, u32[]{:S(2)}) copy-start(f32[512,2,8,16]{0,3,2,1:T(8,128)} %copy-done.12) | copy-start | bytes 1572868
  655.4 46.9 %copy-start.20 = (f32[512,16,2,8]{0,1,3,2:T(8,128)S(1)}, f32[512,16,2,8]{0,1,3,2:T(8,128)}, u32[]{:S(2)}) copy-start(f32[512,16,2,8]{0,1,3,2:T(8,128)} %copy.131) | copy-start | bytes 1572868
  655.4 46.9 %copy-start.25 = (f32[8,512,16]{1,2,0:T(8,128)S(1)}, f32[8,512,16]{1,2,0:T(8,128)}, u32[]{:S(2)}) copy-start(f32[8,512,16]{1,2,0:T(8,128)} %copy.134) | copy-start | bytes 786436
  655.4 46.9 %copy-start.27 = (f32[1,8,512]{2,1,0:T(8,128)S(1)}, f32[1,8,512]{2,1,0:T(8,128)}, u32[]{:S(2)}) copy-start(f32[1,8,512]{2,1,0:T(8,128)} %copy-done.26) | copy-start | bytes 49156
  655.4 47.3 %copy-start.19 = (f32[8,512]{0,1:T(8,128)S(1)}, f32[8,512]{0,1:T(8,128)}, u32[]{:S(2)}) copy-start(f32[8,512]{0,1:T(8,128)} %copy-done.18) | copy-start | bytes 49156
  754.2 6.0 copy-start.15
Sparse Core Ops, SparseCore 0:
  32.6 230.3 all-gather.3
  265.1 225.4 all-gather.5
  492.7 47.2 all-gather.7
  543.2 69.5 all-reduce.3
  702.8 30.7 all-reduce.5
